TPU v7x, 32 devices: a whole 2x2x4 slice. The times are simulated.
32 devices in a mesh: groups: 2 (over x), pairs: 8 (over z, y), mp: 2 (over core).
Axes of the slice: x: 2, y: 2, z: 4, core: 2. Of those that a mesh axis runs over, the one named last changes fastest.
Arguments:
- tokens: bfloat16 [64, 196, 768], P(('groups', 'pairs'), None, 'mp'), parts along dimension 0, may hold values from -6 to 6
- gain_query: float32 [768], replicated, may hold values from 0.25 to 1.75
- gain_context: float32 [768], replicated, may hold values from 0.25 to 1.75
- query_weight: bfloat16 [768, 768], replicated, may hold values from -1 to 1
- key_weight: bfloat16 [768, 768], replicated, may hold values from -8 to 8
- value_weight: bfloat16 [768, 768], replicated, may hold values from -0.21875 to 0.21875
- out_weight: bfloat16 [768, 768], replicated, may hold values from -0.21875 to 0.21875
- gain_head: float32 [768], replicated, may hold values from 0.25 to 1.75
- hidden_weight: bfloat16 [768, 1024], replicated, may hold values from -0.21875 to 0.21875
- hidden_bias: float32 [1024], replicated, may hold values from -3 to 3
- point_weight: bfloat16 [4, 1024], replicated, may hold values from -0.1875 to 0.1875
- view_owner: int32 [192, 1], P('groups'), parts along dimension 0, may hold values from 0 to 7; in each aligned block of 12 rows (0 to 11, 12 to 23, ...) at most 2 rows name the same one
- view_local: int32 [192], P('groups'), parts along dimension 0, may hold values from 0 to 3
- pair_count: int32 [16], P('groups'), parts along dimension 0, may hold values from 1 to 6, 24 in all
Outputs:
- joined: float32 [64, 4, 196], P(('groups', 'pairs', 'mp')), parts along dimension 0
There are 2 independent parts, one for each index of `groups`. A program takes and returns all parts, laid end to end along the dimension named above; an argument that names none is the same for every part. Nothing has to cross between parts.
Inputs may be any that keep to these rules, and one draw needn't show every extreme that they name: `view_owner`: among the 12 views of one worker no owner appears more than 2 times, and in every draw some owner appears exactly 2 times. `pair_count`: some worker has exactly 6 pairs in every draw; the counts sum to 24.
All inputs are finite; a program needn't handle non-finite values.
Results may differ from a plain program's by a relative error of at most 0.012.
The roundings to bfloat16 on the way count: a program that leaves them out, or rounds other values in their place, can miss the bound.
Values may be sent and summed in bfloat16 or wider, within the bound.
No kernel may reach another device: no remote copies, remote signals or barrier semaphores. Data moves between devices by JAX's collectives and lax.ppermute only.
A program may use at most 128 MiB of HBM per device.

v0:
```python
import math
import jax
import jax.numpy as jnp
from jax import lax
from jax.sharding import PartitionSpec as P

HEADS = 12
EPS = 1e-06


def norm_rows(rows_in, gain_vec):
    rows_in = rows_in.astype(jnp.float32)
    average = jnp.mean(rows_in, axis=-1, keepdims=True)
    centered = rows_in - average
    variance = jnp.mean(centered * centered, axis=-1, keepdims=True)
    return (centered * lax.rsqrt(variance + EPS) * gain_vec).astype(jnp.bfloat16)


def project(rows_in, weight):
    return jnp.einsum("vtd,de->vte", rows_in, weight, preferred_element_type=jnp.float32)


def attention(queries, key_rows, value_rows, head_count):
    view_count, token_count, feature_width = queries.shape
    head_size = feature_width // head_count
    split_shape = (view_count, token_count, head_count, head_size)
    scores = jnp.einsum(
        "vqhd,vkhd->vhqk",
        queries.reshape(split_shape),
        key_rows.reshape(split_shape),
        preferred_element_type=jnp.float32,
    ) / math.sqrt(head_size)
    row_max = jnp.max(scores, axis=-1, keepdims=True)
    exponent = jnp.exp(scores - row_max)
    attn_probs = (exponent / jnp.sum(exponent, axis=-1, keepdims=True)).astype(jnp.bfloat16)
    blended = jnp.einsum(
        "vhqk,vkhd->vqhd",
        attn_probs,
        value_rows.reshape(split_shape),
        preferred_element_type=jnp.float32,
    )
    return blended.astype(jnp.bfloat16).reshape(view_count, token_count, feature_width)


def point_terms(head_out):
    confidence = 1.0 + jnp.exp(head_out[:, 3:4])
    return jnp.concatenate([head_out[:, :3] * confidence, confidence], axis=1)


def per_device(
    tokens,
    gain_query,
    gain_context,
    query_weight,
    key_weight,
    value_weight,
    out_weight,
    gain_head,
    hidden_weight,
    hidden_bias,
    point_weight,
    view_owner,
    view_local,
    pair_count,
):
    worker_count = lax.axis_size("pairs")
    worker_index = lax.axis_index("pairs")
    core_index = lax.axis_index("mp")
    core_count = lax.axis_size("mp")
    image_count = tokens.shape[0]
    token_count = tokens.shape[1]
    full_width = query_weight.shape[0]
    hidden_width = hidden_weight.shape[1]
    request_count = view_local.shape[0] // worker_count
    slot_count = request_count // 2
    owners = view_owner[:, 0].reshape(worker_count, request_count)
    local_rows = view_local.reshape(worker_count, request_count)
    global_rows = owners * image_count + local_rows
    my_images = global_rows[worker_index]
    shard_rows = lax.all_gather(tokens, "pairs", axis=0, tiled=True)
    row_ids = jnp.arange(shard_rows.shape[0])
    onehot = (my_images[:, None] == row_ids[None, :]).astype(jnp.bfloat16)
    half_views = jnp.einsum(
        "vi,itd->vtd", onehot, shard_rows, preferred_element_type=jnp.float32
    ).astype(jnp.bfloat16)
    full_views = lax.all_gather(half_views, "mp", axis=2, tiled=True)
    pair_total = pair_count[worker_index]
    part_width = full_width // core_count
    hidden_part = hidden_width // core_count
    context_views = full_views.reshape(slot_count, 2, token_count, full_width)[:, ::-1].reshape(
        request_count, token_count, full_width
    )
    query_in = norm_rows(full_views, gain_query)
    context_in = norm_rows(context_views, gain_context)
    query_part = lax.dynamic_slice_in_dim(query_weight, core_index * part_width, part_width, 1)
    key_part = lax.dynamic_slice_in_dim(key_weight, core_index * part_width, part_width, 1)
    value_part = lax.dynamic_slice_in_dim(value_weight, core_index * part_width, part_width, 1)
    query_proj = project(query_in, query_part).astype(jnp.bfloat16)
    key_proj = project(context_in, key_part).astype(jnp.bfloat16)
    value_proj = project(context_in, value_part).astype(jnp.bfloat16)
    attended_part = attention(query_proj, key_proj, value_proj, HEADS // core_count)
    attended = lax.all_gather(attended_part, "mp", axis=2, tiled=True)
    updated = full_views.astype(jnp.float32) + project(attended, out_weight)
    head_in = norm_rows(updated, gain_head)
    first_part = lax.dynamic_slice_in_dim(hidden_weight, core_index * hidden_part, hidden_part, 1)
    bias_part = lax.dynamic_slice_in_dim(hidden_bias, core_index * hidden_part, hidden_part, 0)
    second_part = lax.dynamic_slice_in_dim(point_weight, core_index * hidden_part, hidden_part, 1)
    hidden = jax.nn.gelu(project(head_in, first_part) + bias_part).astype(jnp.bfloat16)
    head_part = jnp.einsum("vth,ch->vct", hidden, second_part, preferred_element_type=jnp.float32)
    head_out = lax.psum(head_part, "mp")
    view_ids = jnp.arange(request_count)
    live_mask = jnp.logical_and(view_ids % 2 == core_index, view_ids // 2 < pair_total).astype(
        jnp.float32
    )
    contrib = point_terms(head_out) * live_mask[:, None, None]
    image_rows = my_images[view_ids]
    row_ids = jnp.arange(image_count // core_count * lax.axis_size(("pairs", "mp")))
    onehot = (image_rows[:, None] == row_ids[None, :]).astype(jnp.float32)
    return lax.psum_scatter(
        jnp.einsum("vr,vct->rct", onehot, contrib, precision=lax.Precision.HIGHEST),
        ("pairs", "mp"),
        scatter_dimension=0,
        tiled=True,
    )


def solution(mesh):
    return jax.shard_map(
        per_device,
        mesh=mesh,
        in_specs=(
            P(("groups", "pairs"), None, "mp"),
            P(),
            P(),
            P(),
            P(),
            P(),
            P(),
            P(),
            P(),
            P(),
            P(),
            P("groups", None),
            P("groups"),
            P("groups"),
        ),
        out_specs=P(("groups", "pairs", "mp"), None, None),
        check_vma=False,
    )
```

profile of v0, /device:TPU:8, one launch (start us, length us, event | category | flops | bytes accessed | tf_op | source)
XLA Modules:
  0.0 323.9 jit_solution(13960240500838489043)
XLA Ops:
  6.5 0.0 copy-start
  6.5 0.0 all-gather.4.cloned.1.call-start
  6.5 2.1 copy.39
  8.6 0.0 all-gather.4.cloned.1.call-update
  8.7 0.0 all-gather.6.cloned.1.call-start
  8.7 0.7 multiply_reduce_fusion.3
  9.4 0.1 mul.118
  9.5 0.7 reshape.108
  10.2 81.8 %all-gather.4.cloned.1.call-done = bf16[32,196,384]{2,1,0:T(8,128)(2,1)} async-done(((bf16[4,196,384]{2,1,0:T(8,128)(2,1)}), bf16[32,196,384]{2,1,0:T(8,128)(2,1)}) %all-gather.4.cloned.1.call-update) | async-done | bytes 4816912 | tf_op jit(solution)/shard_map/all_gather | solution.py:80
  92.0 4.7 %fusion.31 = bf16[12,196,384]{2,0,1:T(8,128)(2,1)} fusion(bf16[32,196,384]{2,1,0:T(8,128)(2,1)} %all-gather.4.cloned.1.call-done, s32[12]{0:T(128)S(1)} %fusion.77), kind=kOutput, calls=%fused_computation.41 | convolution fusion | flops 58706304 | bytes 6623280 | tf_op jit(solution)/shard_map/vi,itd->vtd/dot_general | solution.py:83
  96.7 0.0 all-gather.6.cloned.1.call-update
  96.8 0.0 all-gather.8.cloned.1.call-start
  96.8 14.0 %all-gather.6.cloned.1.call-done = bf16[12,196,768]{2,0,1:T(8,128)(2,1)} async-done(((bf16[12,196,384]{2,0,1:T(8,128)(2,1)}), bf16[12,196,768]{2,0,1:T(8,128)(2,1)}) %all-gather.6.cloned.1.call-update) | async-done | bytes 3612688 | tf_op jit(solution)/shard_map/all_gather | solution.py:86
  110.8 3.5 %copy.41 = bf16[12,196,768]{2,1,0:T(8,128)(2,1)S(1)} copy(bf16[12,196,768]{2,0,1:T(8,128)(2,1)} %all-gather.6.cloned.1.call-done) | data formatting | bytes 7225344 | tf_op jit(solution)/shard_map/all_gather | solution.py:86
  114.3 0.0 copy-start.1
  114.3 0.6 convert_reduce_fusion.1
  114.9 1.2 copy-done.1
  116.1 1.4 multiply_reduce_fusion.2
  117.5 0.0 copy-start.2
  117.5 3.2 convert_reduce_fusion
  120.7 4.1 %fusion.6 = f32[12,196]{0,1:T(8,128)S(1)} fusion(bf16[12,196,768]{2,0,1:T(8,128)(2,1)} %all-gather.6.cloned.1.call-done, f32[12,196]{0,1:T(8,128)S(1)} %broadcast_multiply_fusion.1), kind=kLoop, calls=%fused_computation.11 | loop fusion | flops 7222992 | bytes 3631488 | tf_op jit(solution)/shard_map/reduce_sum | solution.py:15
  124.8 0.7 add_rsqrt_fusion.1
  125.5 2.8 fusion.11
  128.3 0.0 copy-start.6
  128.3 3.3 %convolution_convert_fusion = bf16[12,196,384]{2,1,0:T(8,128)(2,1)S(1)} fusion(bf16[12,196,768]{2,1,0:T(8,128)(2,1)S(1)} %fusion.11, bf16[768,768]{1,0:T(8,128)(2,1)} %param.18, s32[]{:T(128)S(6)} %select_n.37), kind=kOutput, calls=%fused_computation.44 | convolution fusion | flops 1388169216 | bytes 6008836 | tf_op jit(solution)/shard_map/vtd,de->vte/dot_general | solution.py:20
  131.7 3.4 %convolution_convert_fusion.1 = bf16[12,196,384]{2,1,0:T(8,128)(2,1)} fusion(bf16[12,196,768]{2,1,0:T(8,128)(2,1)S(1)} %fusion.11, bf16[768,768]{1,0:T(8,128)(2,1)S(1)} %copy-done.6, s32[]{:T(128)S(6)} %select_n.37), kind=kOutput, calls=%fused_computation.45 | convolution fusion | flops 1388169216 | bytes 6082564 | tf_op jit(solution)/shard_map/vtd,de->vte/dot_general | solution.py:20
  135.1 4.0 %copy.42 = bf16[12,196,384]{1,2,0:T(8,128)(2,1)} copy(bf16[12,196,384]{2,1,0:T(8,128)(2,1)} %convolution_convert_fusion.1) | data formatting | bytes 3612672 | tf_op jit(solution)/shard_map/convert_element_type | solution.py:100
  139.2 2.5 copy.45
  141.6 4.3 %fusion.8 = bf16[12,196,768]{2,0,1:T(8,128)(2,1)S(1)} fusion(bf16[12,196,768]{2,0,1:T(8,128)(2,1)} %all-gather.6.cloned.1.call-done, f32[768]{0:T(1024)S(1)} %copy-done.3, f32[12,196]{0,1:T(8,128)} %add_rsqrt_fusion.1, f32[12,196]{0,1:T(8,128)S(1)} %broadcast_multiply_fusion.1), kind=kLoop, calls=%fused_computation.13 | loop fusion | flops 9031680 | bytes 7247232 | tf_op jit(solution)/shard_map/convert_element_type | solution.py:16
  145.9 0.0 copy-done.7
  145.9 2.9 fusion.35
  148.9 2.5 copy.44
  151.4 13.0 %fusion.83 = (f32[12,6,196]{2,1,0:T(8,128)S(1)}, f32[12,6,196,196]{2,3,1,0:T(8,128)}) fusion(bf16[12,196,6,64]{1,3,2,0:T(8,128)(2,1)} %bitcast.64, bf16[12,196,6,64]{1,3,2,0:T(8,128)(2,1)} %bitcast.63), kind=kOutput, calls=%fused_computation.98 | convolution fusion | flops 362339904 | bytes 14732928 | tf_op jit(solution)/shard_map/sub | solution.py:34
  164.4 8.9 %fusion.34 = bf16[12,6,64,196]{3,2,1,0:T(8,128)(2,1)} fusion(bf16[12,196,6,64]{1,3,2,0:T(8,128)(2,1)} %bitcast.62, f32[12,6,196,196]{2,3,1,0:T(8,128)} %get-tuple-element.6, f32[12,6,196]{2,1,0:T(8,128)S(1)} %get-tuple-element.5), kind=kOutput, calls=%fused_computation.42 | convolution fusion | flops 360476928 | bytes 14732928 | tf_op jit(solution)/shard_map/vhqk,vkhd->vqhd/dot_general | solution.py:36
  173.3 4.2 %copy.47 = bf16[12,196,384]{2,1,0:T(8,128)(2,1)} copy(bf16[12,196,384]{1,2,0:T(8,128)(2,1)} %bitcast.65) | data formatting | bytes 3612672 | tf_op jit(solution)/shard_map/reshape | solution.py:42
  177.5 0.0 all-gather.8.cloned.1.call-update
  177.5 0.0 all-reduce.3.cloned.1.call-start
  177.6 0.6 dynamic_slice.31
  178.2 0.7 gather_fusion
  178.8 0.1 dynamic_slice.30
  178.9 0.6 and_convert_fusion
  179.6 12.1 %all-gather.8.cloned.1.call-done = bf16[12,196,768]{2,1,0:T(8,128)(2,1)} async-done(((bf16[12,196,384]{2,1,0:T(8,128)(2,1)}), bf16[12,196,768]{2,1,0:T(8,128)(2,1)}) %all-gather.8.cloned.1.call-update) | async-done | bytes 3612688 | tf_op jit(solution)/shard_map/all_gather | solution.py:102
  191.7 0.0 copy-done.8
  191.7 5.2 %fusion.44 = f32[12,196,768]{2,1,0:T(8,128)S(1)} fusion(bf16[12,196,768]{2,1,0:T(8,128)(2,1)} %all-gather.8.cloned.1.call-done, bf16[768,768]{1,0:T(8,128)(2,1)S(1)} %copy-done.8), kind=kOutput, calls=%fused_computation.47 | convolution fusion | flops 2774532096 | bytes 12017664 | tf_op jit(solution)/shard_map/vtd,de->vte/dot_general | solution.py:20
  196.9 0.0 slice-start
  196.9 4.7 %fusion.24 = f32[12,196]{0,1:T(8,128)S(1)} fusion(f32[12,196,768]{2,1,0:T(8,128)S(1)} %fusion.44, bf16[12,196,768]{2,0,1:T(8,128)(2,1)} %all-gather.6.cloned.1.call-done), kind=kLoop, calls=%fused_computation.34 | loop fusion | flops 5416656 | bytes 10847424 | tf_op jit(solution)/shard_map/reduce_sum | solution.py:13
  201.6 0.0 slice-start.1
  201.6 0.0 copy-start.4
  201.6 7.0 %multiply_reduce_fusion.1 = f32[12,196]{0,1:T(8,128)S(1)} fusion(f32[12,196]{0,1:T(8,128)S(1)} %broadcast_multiply_fusion, f32[12,196,768]{2,1,0:T(8,128)S(1)} %fusion.44, bf16[12,196,768]{2,0,1:T(8,128)(2,1)} %all-gather.6.cloned.1.call-done), kind=kLoop, calls=%fused_computation.15 | loop fusion | flops 9029328 | bytes 10856832 | tf_op jit(solution)/shard_map/reduce_sum | solution.py:15
  208.7 0.0 slice-done
  208.7 0.0 slice-done.1
  208.7 0.0 copy-done.4
  208.7 0.0 copy-start.9
  208.7 5.1 %multiply_convert_fusion = bf16[12,196,768]{2,0,1:T(8,128)(2,1)} fusion(f32[768]{0:T(1024)S(1)} %copy-done.4, f32[12,196]{0,1:T(8,128)S(1)} %add_rsqrt_fusion, f32[12,196]{0,1:T(8,128)S(1)} %broadcast_multiply_fusion, f32[12,196,768]{2,1,0:T(8,128)S(1)} %fusion.44, bf16[12,196,768]{2,0,1:T(8,128)(2,1)S(1)} %bitcast.58), kind=kLoop, calls=%fused_computation.14 | loop fusion | flops 10838016 | bytes 14472576 | tf_op jit(solution)/shard_map/convert_element_type | solution.py:16
  213.9 0.0 copy-done
  213.9 6.7 %fusion.46 = f32[12,4,196]{2,1,0:T(4,128)S(1)} fusion(f32[512]{0:T(512)S(1)} %dynamic_slice.30, bf16[12,196,768]{2,0,1:T(8,128)(2,1)} %multiply_convert_fusion, bf16[768,1024]{1,0:T(8,128)(2,1)S(1)} %copy-done, s32[]{:T(128)S(6)} %select_n.36, bf16[4,1024]{1,0:T(4,128)(2,1)S(1)} %copy-done.9), kind=kOutput, calls=%fused_computation.49 | convolution fusion | flops 1871364096 | bytes 4443904 | tf_op jit(solution)/shard_map/vth,ch->vct/dot_general | solution.py:109
  220.6 3.7 %psum.7 = f32[12,4,196]{2,1,0:T(4,128)S(1)} all-reduce(f32[12,4,196]{2,1,0:T(4,128)S(1)} %fusion.46), channel_id=1, replica_groups=mesh['groups'=2,'pairs'=8,'mp'=2] {'mp'}, use_global_device_ids=true, to_apply=%region_8.0 | all-reduce | flops 9408 | bytes 75264 | tf_op jit(solution)/shard_map/psum | solution.py:110
  224.3 0.1 maximum_multiply_fusion
  224.4 0.3 fusion.61
  224.7 0.7 copy.51
  225.4 0.0 all-reduce.3.cloned.1.call-update
  225.5 0.6 dynamic-slice
  226.7 89.4 %all-reduce.3.cloned.1.call-done = f32[32,4,196]{2,1,0:T(4,128)} async-done(((f32[32,4,196]{2,1,0:T(4,128)}), f32[32,4,196]{2,1,0:T(4,128)}) %all-reduce.3.cloned.1.call-update) | async-done | bytes 100368
  316.1 1.3 constant_dynamic-slice_fusion.1
  (28 shorter events, 0.2 us)
Async XLA Ops:
  6.5 207.3 %copy-start = (bf16[768,1024]{1,0:T(8,128)(2,1)S(1)}, bf16[768,1024]{1,0:T(8,128)(2,1)}, u32[]{:S(2)}) copy-start(bf16[768,1024]{1,0:T(8,128)(2,1)} %param.22) | copy-start | bytes 4718596
  6.5 85.5 %all-gather.4.cloned.1.call-start = ((), (), s32[]{:S(2)}) async-start(), calls=%async_computation | async-start | bytes 5529600 | tf_op jit(solution)/shard_map/all_gather | solution.py:80
  8.7 102.1 %all-gather.6.cloned.1.call-start = ((), (), s32[]{:S(2)}) async-start(), calls=%async_computation.1 | async-start | bytes 7225344 | tf_op jit(solution)/shard_map/all_gather | solution.py:86
  96.8 94.9 %all-gather.8.cloned.1.call-start = ((), (), s32[]{:S(2)}) async-start(), calls=%async_computation.2 | async-start | bytes 5529600 | tf_op jit(solution)/shard_map/all_gather | solution.py:102
  114.3 1.8 copy-start.1
  117.5 8.1 %copy-start.2 = (f32[768]{0:T(1024)S(1)}, f32[768]{0:T(1024)}, u32[]{:S(2)}) copy-start(f32[768]{0:T(1024)} %param.16) | copy-start | bytes 9220
  128.3 3.3 %copy-start.6 = (bf16[768,768]{1,0:T(8,128)(2,1)S(1)}, bf16[768,768]{1,0:T(8,128)(2,1)}, u32[]{:S(2)}) copy-start(bf16[768,768]{1,0:T(8,128)(2,1)} %param.19) | copy-start | bytes 3538948
  135.1 6.5 %copy-start.3 = (f32[768]{0:T(1024)S(1)}, f32[768]{0:T(1024)}, u32[]{:S(2)}) copy-start(f32[768]{0:T(1024)} %param.15) | copy-start | bytes 9220
  141.6 4.3 %copy-start.7 = (bf16[768,768]{1,0:T(8,128)(2,1)S(1)}, bf16[768,768]{1,0:T(8,128)(2,1)}, u32[]{:S(2)}) copy-start(bf16[768,768]{1,0:T(8,128)(2,1)} %param.17) | copy-start | bytes 3538948
  173.3 4.3 %copy-start.10 = (s32[8]{0:T(128)S(1)}, s32[8]{0:T(128)}, u32[]{:S(2)}) copy-start(s32[8]{0:T(128)} %param.27) | copy-start | bytes 100
  173.3 5.5 %copy-start.5 = (f32[1024]{0:T(1024)S(1)}, f32[1024]{0:T(1024)}, u32[]{:S(2)}) copy-start(f32[1024]{0:T(1024)} %param.23) | copy-start | bytes 12292
  173.3 18.4 %copy-start.8 = (bf16[768,768]{1,0:T(8,128)(2,1)S(1)}, bf16[768,768]{1,0:T(8,128)(2,1)}, u32[]{:S(2)}) copy-start(bf16[768,768]{1,0:T(8,128)(2,1)} %param.20) | copy-start | bytes 3538948
  177.5 138.6 %all-reduce.3.cloned.1.call-start = ((), (), s32[]{:S(2)}) async-start(), calls=%async_computation.3 | async-start | bytes 262144
  196.9 11.8 %slice-start = ((s8[4816896]{0:T(1024)(128)(4,1)}), s8[622592]{0:T(1024)(128)(4,1)S(1)}, s32[]{:S(2)}) async-start(s8[4816896]{0:T(1024)(128)(4,1)} %bitcast.57), calls=%async_computation.4 | async-start | bytes 1245184
  201.6 7.1 %slice-start.1 = ((s8[4816896]{0:T(1024)(128)(4,1)}), s8[4194304]{0:T(1024)(128)(4,1)S(1)}, s32[]{:S(2)}) async-start(s8[4816896]{0:T(1024)(128)(4,1)} %bitcast.57), calls=%async_computation.5 | async-start | bytes 8388608
  201.6 7.1 %copy-start.4 = (f32[768]{0:T(1024)S(1)}, f32[768]{0:T(1024)}, u32[]{:S(2)}) copy-start(f32[768]{0:T(1024)} %param.21) | copy-start | bytes 9220
  208.7 5.2 %copy-start.9 = (bf16[4,1024]{1,0:T(4,128)(2,1)S(1)}, bf16[4,1024]{1,0:T(4,128)(2,1)}, u32[]{:S(2)}) copy-start(bf16[4,1024]{1,0:T(4,128)(2,1)} %param.24) | copy-start | bytes 24580
  213.9 11.6 %copy-start.11 = (u32[32]{0:T(128)S(1)}, u32[32]{0:T(128)}, u32[]{:S(2)}) copy-start(u32[32]{0:T(128)} %constant.82) | copy-start | bytes 388
Sparse Core Ops, SparseCore 0:
  9.5 82.4 all-gather.3
  96.9 13.8 all-gather.5
  177.6 14.0 all-gather.7
  225.6 90.4 all-reduce.2
where the time goes:
time: 325 us; the launch traced here: 324 us
  waiting for transfers between devices  197 us (61%)
  matrix products  48.5 us (15%)
  other arithmetic  35.4 us (11%)
  local copies, waits for them, and re-layouts  24.9 us (8%)
  between operations  14.1 us (4%)
  blocking collectives  3.65 us (1%)
    unnamed x5, waiting for transfers between devices  89.4 us
    all_gather x1, waiting for transfers between devices, per_device(): shard_rows = lax.all_gather(tokens, 'pairs', axis=0, tiled=True)  81.8 us
    dot_general x4, matrix products, project(): jnp.einsum('vtd,de->vte', rows_in, weight, preferred_element_type=jnp.flo...  14.9 us
    all_gather x1, waiting for transfers between devices, per_device(): full_views = lax.all_gather(half_views, 'mp', axis=2, tiled=True)  14 us
    sub x1, matrix products, attention(): exponent = jnp.exp(scores - row_max)  13 us
    reduce_sum x3, other arithmetic, norm_rows(): variance = jnp.mean(centered * centered, axis=-1, keepdims=True)  12.5 us
    convert_element_type x3, other arithmetic, norm_rows(): (centered * lax.rsqrt(variance + EPS) * gain_vec).astype(jnp.bfloat16)  12.2 us
    all_gather x1, waiting for transfers between devices, per_device(): attended = lax.all_gather(attended_part, 'mp', axis=2, tiled=True)  12.1 us
  transfers between devices with their start and end apart: 4, of which 4 were waited for; matrix products, arithmetic and copies ran while one was open for 1% of the time, Pallas kernels for 0%

commit v1 on v0

--- a/solution.py
+++ b/solution.py
@@ -6,6 +6,22 @@
 
 HEADS = 12
 EPS = 1e-06
+
+
+def collect(x, axis, dim):
+    ways, here, step = (lax.axis_size(axis), lax.axis_index(axis), x.shape[dim])
+    lengths = [n * ways if d == dim else n for d, n in enumerate(x.shape)]
+    full = lax.dynamic_update_slice_in_dim(jnp.zeros(lengths, x.dtype), x, here * step, axis=dim)
+    going_up = going_down = x
+    for far in range(1, ways // 2 + 1):
+        going_up = lax.ppermute(going_up, axis, [(d, (d + 1) % ways) for d in range(ways)])
+        full = lax.dynamic_update_slice_in_dim(full, going_up, (here - far) % ways * step, axis=dim)
+        if 2 * far < ways:
+            going_down = lax.ppermute(going_down, axis, [(d, (d - 1) % ways) for d in range(ways)])
+            full = lax.dynamic_update_slice_in_dim(
+                full, going_down, (here + far) % ways * step, axis=dim
+            )
+    return full
 
 
 def norm_rows(rows_in, gain_vec):
@@ -77,7 +93,7 @@
     local_rows = view_local.reshape(worker_count, request_count)
     global_rows = owners * image_count + local_rows
     my_images = global_rows[worker_index]
-    shard_rows = lax.all_gather(tokens, "pairs", axis=0, tiled=True)
+    shard_rows = collect(tokens, "pairs", 0)
     row_ids = jnp.arange(shard_rows.shape[0])
     onehot = (my_images[:, None] == row_ids[None, :]).astype(jnp.bfloat16)
     half_views = jnp.einsum(

time: 325 us -> 341 us (1.049); the launches traced: 324 us -> 335 us
  starting transfers between devices: 0.13 us -> 11.3 us
  local copies, waits for them, and re-layouts: 24.9 us -> 28.8 us
    all_gather x1 -> x0, waiting for transfers between devices: 81.8 us -> none  [per_device(): shard_rows = lax.all_gather(tokens, 'pairs', axis=0, tiled=True)]
    ppermute x0 -> x7, waiting for transfers between devices: none -> 77.3 us  [the longest x4 77.3 us: collect(): lax.ppermute(going_up, axis, [(d, (d + 1) % ways) for d in range(ways)])]
    ppermute x0 -> x7, starting transfers between devices: none -> 11.2 us  [the longest x4 8.86 us: collect(): lax.ppermute(going_up, axis, [(d, (d + 1) % ways) for d in range(ways)])]
    dynamic_update_slice x0 -> x8, local copies, waits for them, and re-layouts: none -> 5.48 us  [the longest x4 2.74 us: collect(): lax.dynamic_update_slice_in_dim(full, going_up, (here - far) % ways * ste...]
    unnamed x5 -> x4, waiting for transfers between devices: 89.4 us -> 89.3 us
  transfers between devices with their start and end apart: 4 -> 10, of which waited for: 4 -> 7; matrix products, arithmetic and copies ran while one was open for 1% -> 3% of each run, Pallas kernels for 0% -> 0%
where the time goes in v1:
time: 341 us; the launch traced here: 335 us
  waiting for transfers between devices  195 us (57%)
  matrix products  46.1 us (14%)
  other arithmetic  35.7 us (10%)
  local copies, waits for them, and re-layouts  28.8 us (8%)
  between operations  14.4 us (4%)
  starting transfers between devices  11.3 us (3%)
  blocking collectives  3.65 us (1%)
    unnamed x4, waiting for transfers between devices  89.3 us
    ppermute x4, waiting for transfers between devices, collect(): lax.ppermute(going_up, axis, [(d, (d + 1) % ways) for d in range(ways)])  77.3 us
    all_gather x1, waiting for transfers between devices, per_device(): full_views = lax.all_gather(half_views, 'mp', axis=2, tiled=True)  15.8 us
    dot_general x4, matrix products, project(): jnp.einsum('vtd,de->vte', rows_in, weight, preferred_element_type=jnp.flo...  14.9 us
    sub x1, matrix products, attention(): exponent = jnp.exp(scores - row_max)  13 us
    reduce_sum x3, other arithmetic, norm_rows(): variance = jnp.mean(centered * centered, axis=-1, keepdims=True)  12.9 us
    convert_element_type x3, other arithmetic, norm_rows(): (centered * lax.rsqrt(variance + EPS) * gain_vec).astype(jnp.bfloat16)  12.2 us
    all_gather x1, waiting for transfers between devices, per_device(): attended = lax.all_gather(attended_part, 'mp', axis=2, tiled=True)  12.1 us
  transfers between devices with their start and end apart: 10, of which 7 were waited for; matrix products, arithmetic and copies ran while one was open for 3% of the time, Pallas kernels for 0%

profile of v1, /device:TPU:8, one launch (start us, length us, event | category | flops | bytes accessed | tf_op | source)
XLA Modules:
  0.0 334.6 jit_solution(3713429233908504908)
XLA Ops:
  6.5 1.5 collective-permute-start
  8.1 1.4 collective-permute-start.1
  9.5 24.7 %collective-permute-done = bf16[4,196,384]{2,0,1:T(4,128)(2,1)S(1)} collective-permute-done((bf16[4,196,384]{2,0,1:T(4,128)(2,1)}, bf16[4,196,384]{2,0,1:T(4,128)(2,1)S(1)}, u32[]{:S(2)}, u32[]{:S(2)}) %collective-permute-start) | collective-permute-done | bytes 602144 | tf_op jit(solution)/shard_map/ppermute | solution.py:17
  34.1 2.4 collective-permute-start.2
  36.5 0.5 collective-permute-start.3
  37.1 24.3 %collective-permute-done.2 = bf16[4,196,384]{2,0,1:T(4,128)(2,1)} collective-permute-done((bf16[4,196,384]{2,0,1:T(4,128)(2,1)S(1)}, bf16[4,196,384]{2,0,1:T(4,128)(2,1)}, u32[]{:S(2)}, u32[]{:S(2)}) %collective-permute-start.2) | collective-permute-done | bytes 602144 | tf_op jit(solution)/shard_map/ppermute | solution.py:17
  61.4 2.6 collective-permute-start.4
  64.0 0.7 multiply_reduce_fusion.3
  64.7 0.1 mul.142
  64.7 0.7 reshape.108
  65.5 0.4 broadcast_in_dim.2
  65.9 0.4 constant_dynamic-update-slice_fusion.7
  66.4 0.4 collective-permute-start.5
  66.8 0.4 constant_dynamic-update-slice_fusion.6
  67.2 21.3 %collective-permute-done.4 = bf16[4,196,384]{2,0,1:T(4,128)(2,1)S(1)} collective-permute-done((bf16[4,196,384]{2,0,1:T(4,128)(2,1)}, bf16[4,196,384]{2,0,1:T(4,128)(2,1)S(1)}, u32[]{:S(2)}, u32[]{:S(2)}) %collective-permute-start.4) | collective-permute-done | bytes 602144 | tf_op jit(solution)/shard_map/ppermute | solution.py:17
  88.5 2.4 collective-permute-start.6
  90.8 0.4 constant_dynamic-update-slice_fusion.5
  91.3 1.5 constant_dynamic-update-slice_fusion.4
  92.8 1.5 constant_dynamic-update-slice_fusion.3
  94.3 0.4 constant_dynamic-update-slice_fusion.2
  94.7 0.4 constant_dynamic-update-slice_fusion.1
  95.1 7.0 %collective-permute-done.6 = bf16[4,196,384]{2,0,1:T(4,128)(2,1)S(1)} collective-permute-done((bf16[4,196,384]{2,0,1:T(4,128)(2,1)S(1)}, bf16[4,196,384]{2,0,1:T(4,128)(2,1)S(1)}, u32[]{:S(2)}, u32[]{:S(2)}) %collective-permute-start.6) | collective-permute-done | bytes 602144 | tf_op jit(solution)/shard_map/ppermute | solution.py:17
  102.1 0.4 constant_dynamic-update-slice_fusion
  102.6 2.3 convolution_convert_fusion
  104.8 0.0 all-gather.5.cloned.1.call-start
  104.9 15.8 %all-gather.3.cloned.1.call-done = bf16[12,196,768]{2,0,1:T(8,128)(2,1)} async-done(((bf16[12,196,384]{2,0,1:T(8,128)(2,1)}), bf16[12,196,768]{2,0,1:T(8,128)(2,1)}) %all-gather.3.cloned.1.call-update) | async-done | bytes 3612688 | tf_op jit(solution)/shard_map/all_gather | solution.py:102
  120.8 3.5 %copy.39 = bf16[12,196,768]{2,1,0:T(8,128)(2,1)S(1)} copy(bf16[12,196,768]{2,0,1:T(8,128)(2,1)} %all-gather.3.cloned.1.call-done) | data formatting | bytes 7225344 | tf_op jit(solution)/shard_map/all_gather | solution.py:102
  124.3 0.6 convert_reduce_fusion.1
  124.9 1.2 copy-done.1
  126.1 1.8 multiply_reduce_fusion.2
  127.9 3.2 convert_reduce_fusion
  131.2 4.1 %fusion.6 = f32[12,196]{0,1:T(8,128)S(1)} fusion(bf16[12,196,768]{2,0,1:T(8,128)(2,1)} %all-gather.3.cloned.1.call-done, f32[12,196]{0,1:T(8,128)S(1)} %broadcast_multiply_fusion.1), kind=kLoop, calls=%fused_computation.11 | loop fusion | flops 7222992 | bytes 3631488 | tf_op jit(solution)/shard_map/reduce_sum | solution.py:31
  135.3 0.7 add_rsqrt_fusion.1
  136.0 2.8 fusion.11
  138.8 3.3 convolution_convert_fusion.1
  142.1 3.4 %convolution_convert_fusion.2 = bf16[12,196,384]{2,1,0:T(8,128)(2,1)} fusion(bf16[12,196,768]{2,1,0:T(8,128)(2,1)S(1)} %fusion.11, bf16[768,768]{1,0:T(8,128)(2,1)S(1)} %copy-done.9, s32[]{:T(128)S(6)} %select_n.106), kind=kOutput, calls=%fused_computation.43 | convolution fusion | flops 1388169216 | bytes 6082564 | tf_op jit(solution)/shard_map/vtd,de->vte/dot_general | solution.py:36
  145.6 4.0 %copy.40 = bf16[12,196,384]{1,2,0:T(8,128)(2,1)} copy(bf16[12,196,384]{2,1,0:T(8,128)(2,1)} %convolution_convert_fusion.2) | data formatting | bytes 3612672 | tf_op jit(solution)/shard_map/convert_element_type | solution.py:116
  149.6 2.5 copy.43
  152.1 4.3 %fusion.8 = bf16[12,196,768]{2,0,1:T(8,128)(2,1)S(1)} fusion(bf16[12,196,768]{2,0,1:T(8,128)(2,1)} %all-gather.3.cloned.1.call-done, f32[768]{0:T(1024)S(1)} %copy-done.6, f32[12,196]{0,1:T(8,128)} %add_rsqrt_fusion.1, f32[12,196]{0,1:T(8,128)S(1)} %broadcast_multiply_fusion.1), kind=kLoop, calls=%fused_computation.13 | loop fusion | flops 9031680 | bytes 7247232 | tf_op jit(solution)/shard_map/convert_element_type | solution.py:32
  156.4 2.9 fusion.30
  159.3 2.6 copy.42
  162.0 13.0 %fusion.78 = (f32[12,6,196]{2,1,0:T(8,128)S(1)}, f32[12,6,196,196]{2,3,1,0:T(8,128)}) fusion(bf16[12,196,6,64]{1,3,2,0:T(8,128)(2,1)} %bitcast.65, bf16[12,196,6,64]{1,3,2,0:T(8,128)(2,1)} %bitcast.64), kind=kOutput, calls=%fused_computation.104 | convolution fusion | flops 362339904 | bytes 14732928 | tf_op jit(solution)/shard_map/sub | solution.py:50
  174.9 9.0 %fusion.29 = bf16[12,6,64,196]{3,2,1,0:T(8,128)(2,1)} fusion(bf16[12,196,6,64]{1,3,2,0:T(8,128)(2,1)} %bitcast.63, f32[12,6,196,196]{2,3,1,0:T(8,128)} %get-tuple-element.6, f32[12,6,196]{2,1,0:T(8,128)S(1)} %get-tuple-element.5), kind=kOutput, calls=%fused_computation.40 | convolution fusion | flops 360476928 | bytes 14732928 | tf_op jit(solution)/shard_map/vhqk,vkhd->vqhd/dot_general | solution.py:52
  183.9 4.2 %copy.45 = bf16[12,196,384]{2,1,0:T(8,128)(2,1)} copy(bf16[12,196,384]{1,2,0:T(8,128)(2,1)} %bitcast.66) | data formatting | bytes 3612672 | tf_op jit(solution)/shard_map/reshape | solution.py:58
  188.1 0.0 all-gather.5.cloned.1.call-update
  188.1 0.0 all-reduce.3.cloned.1.call-start
  188.2 0.6 dynamic_slice.31
  188.8 0.7 gather_fusion
  189.5 0.1 dynamic_slice.30
  189.5 0.6 and_convert_fusion
  190.2 12.1 %all-gather.5.cloned.1.call-done = bf16[12,196,768]{2,1,0:T(8,128)(2,1)} async-done(((bf16[12,196,384]{2,1,0:T(8,128)(2,1)}), bf16[12,196,768]{2,1,0:T(8,128)(2,1)}) %all-gather.5.cloned.1.call-update) | async-done | bytes 3612688 | tf_op jit(solution)/shard_map/all_gather | solution.py:118
  202.3 5.2 %fusion.39 = f32[12,196,768]{2,1,0:T(8,128)S(1)} fusion(bf16[12,196,768]{2,1,0:T(8,128)(2,1)} %all-gather.5.cloned.1.call-done, bf16[768,768]{1,0:T(8,128)(2,1)S(1)} %copy-done.11), kind=kOutput, calls=%fused_computation.45 | convolution fusion | flops 2774532096 | bytes 12017664 | tf_op jit(solution)/shard_map/vtd,de->vte/dot_general | solution.py:36
  207.5 4.7 %fusion.22 = f32[12,196]{0,1:T(8,128)S(1)} fusion(f32[12,196,768]{2,1,0:T(8,128)S(1)} %fusion.39, bf16[12,196,768]{2,0,1:T(8,128)(2,1)} %all-gather.3.cloned.1.call-done), kind=kLoop, calls=%fused_computation.32 | loop fusion | flops 5416656 | bytes 10847424 | tf_op jit(solution)/shard_map/reduce_sum | solution.py:29
  212.3 6.9 %multiply_reduce_fusion.1 = f32[12,196]{0,1:T(8,128)S(1)} fusion(f32[12,196]{0,1:T(8,128)S(1)} %broadcast_multiply_fusion, f32[12,196,768]{2,1,0:T(8,128)S(1)} %fusion.39, bf16[12,196,768]{2,0,1:T(8,128)(2,1)} %all-gather.3.cloned.1.call-done), kind=kLoop, calls=%fused_computation.15 | loop fusion | flops 9029328 | bytes 10856832 | tf_op jit(solution)/shard_map/reduce_sum | solution.py:31
  219.3 5.1 %multiply_convert_fusion = bf16[12,196,768]{2,0,1:T(8,128)(2,1)} fusion(f32[768]{0:T(1024)S(1)} %copy-done.7, f32[12,196]{0,1:T(8,128)S(1)} %add_rsqrt_fusion, f32[12,196]{0,1:T(8,128)S(1)} %broadcast_multiply_fusion, f32[12,196,768]{2,1,0:T(8,128)S(1)} %fusion.39, bf16[12,196,768]{2,0,1:T(8,128)(2,1)S(1)} %bitcast.59), kind=kLoop, calls=%fused_computation.14 | loop fusion | flops 10838016 | bytes 14472576 | tf_op jit(solution)/shard_map/convert_element_type | solution.py:32
  224.4 6.7 %fusion.41 = f32[12,4,196]{2,1,0:T(4,128)S(1)} fusion(f32[512]{0:T(512)S(1)} %dynamic_slice.30, bf16[12,196,768]{2,0,1:T(8,128)(2,1)} %multiply_convert_fusion, bf16[768,1024]{1,0:T(8,128)(2,1)S(1)} %copy-done, s32[]{:T(128)S(6)} %select_n.90, bf16[4,1024]{1,0:T(4,128)(2,1)S(1)} %copy-done.12), kind=kOutput, calls=%fused_computation.47 | convolution fusion | flops 1871364096 | bytes 4443904 | tf_op jit(solution)/shard_map/vth,ch->vct/dot_general | solution.py:125
  231.1 3.6 %psum.7 = f32[12,4,196]{2,1,0:T(4,128)S(1)} all-reduce(f32[12,4,196]{2,1,0:T(4,128)S(1)} %fusion.41), channel_id=1, replica_groups=mesh['groups'=2,'pairs'=8,'mp'=2] {'mp'}, use_global_device_ids=true, to_apply=%region_8.9 | all-reduce | flops 9408 | bytes 75264 | tf_op jit(solution)/shard_map/psum | solution.py:126
  234.8 0.1 maximum_multiply_fusion
  234.9 0.3 fusion.56
  235.2 0.7 copy.49
  236.0 0.0 all-reduce.3.cloned.1.call-update
  236.0 0.6 dynamic-slice
  237.2 89.3 %all-reduce.3.cloned.1.call-done = f32[32,4,196]{2,1,0:T(4,128)} async-done(((f32[32,4,196]{2,1,0:T(4,128)}), f32[32,4,196]{2,1,0:T(4,128)}) %all-reduce.3.cloned.1.call-update) | async-done | bytes 100368
  326.5 1.3 constant_dynamic-slice_fusion.1
  (53 shorter events, 0.3 us)
Async XLA Ops:
  6.5 217.9 %copy-start = (bf16[768,1024]{1,0:T(8,128)(2,1)S(1)}, bf16[768,1024]{1,0:T(8,128)(2,1)}, u32[]{:S(2)}) copy-start(bf16[768,1024]{1,0:T(8,128)(2,1)} %param.22) | copy-start | bytes 4718596
  6.5 59.4 %copy-start.2 = (bf16[4,196,384]{2,0,1:T(4,128)(2,1)S(1)}, bf16[4,196,384]{2,0,1:T(4,128)(2,1)}, u32[]{:S(2)}) copy-start(bf16[4,196,384]{2,0,1:T(4,128)(2,1)} %param.14) | copy-start | bytes 1806340
  6.5 114.2 %all-gather.3.cloned.1.call-start = ((), (), s32[]{:S(2)}) async-start(), calls=%async_computation | async-start | bytes 7225344 | tf_op jit(solution)/shard_map/all_gather | solution.py:102
  6.5 27.6 %collective-permute-start = (bf16[4,196,384]{2,0,1:T(4,128)(2,1)}, bf16[4,196,384]{2,0,1:T(4,128)(2,1)S(1)}, u32[]{:S(2)}, u32[]{:S(2)}) collective-permute-start(bf16[4,196,384]{2,0,1:T(4,128)(2,1)} %param.14), channel_id=1, source_target_pairs={{0,2},{2,4},{4,6},{6,8},{8,10},{10,12},{12,14},{14,0},{1,3},{3,5},... | collective-permute-start | bytes 1806344 | tf_op jit(solution)/shard_map/ppermute | solution.py:17
  8.1 28.4 %collective-permute-start.1 = (bf16[4,196,384]{2,0,1:T(4,128)(2,1)}, bf16[4,196,384]{2,0,1:T(4,128)(2,1)S(1)}, u32[]{:S(2)}, u32[]{:S(2)}) collective-permute-start(bf16[4,196,384]{2,0,1:T(4,128)(2,1)} %param.14), channel_id=1, source_target_pairs={{0,14},{2,0},{4,2},{6,4},{8,6},{10,8},{12,10},{14,12},{1,15},{3,1}... | collective-permute-start | bytes 1806344 | tf_op jit(solution)/shard_map/ppermute | solution.py:20
  34.1 2.9 copy-start.3
  34.1 27.3 %collective-permute-start.2 = (bf16[4,196,384]{2,0,1:T(4,128)(2,1)S(1)}, bf16[4,196,384]{2,0,1:T(4,128)(2,1)}, u32[]{:S(2)}, u32[]{:S(2)}) collective-permute-start(bf16[4,196,384]{2,0,1:T(4,128)(2,1)S(1)} %collective-permute-done), channel_id=1, source_target_pairs={{0,2},{2,4},{4,6},{6,8},{8,10},{10,12},{12,14},{14,0},{1,3},{3,5},... | collective-permute-start | bytes 1806344 | tf_op jit(solution)/shard_map/ppermute | solution.py:17
  36.5 29.8 %collective-permute-start.3 = (bf16[4,196,384]{2,0,1:T(4,128)(2,1)S(1)}, bf16[4,196,384]{2,0,1:T(4,128)(2,1)}, u32[]{:S(2)}, u32[]{:S(2)}) collective-permute-start(bf16[4,196,384]{2,0,1:T(4,128)(2,1)S(1)} %collective-permute-done.1), channel_id=1, source_target_pairs={{0,14},{2,0},{4,2},{6,4},{8,6},{10,8},{12,10},{14,12},{1,15},{3,1}... | collective-permute-start | bytes 1806344 | tf_op jit(solution)/shard_map/ppermute | solution.py:20
  61.4 27.1 %collective-permute-start.4 = (bf16[4,196,384]{2,0,1:T(4,128)(2,1)}, bf16[4,196,384]{2,0,1:T(4,128)(2,1)S(1)}, u32[]{:S(2)}, u32[]{:S(2)}) collective-permute-start(bf16[4,196,384]{2,0,1:T(4,128)(2,1)} %collective-permute-done.2), channel_id=1, source_target_pairs={{0,2},{2,4},{4,6},{6,8},{8,10},{10,12},{12,14},{14,0},{1,3},{3,5},... | collective-permute-start | bytes 1806344 | tf_op jit(solution)/shard_map/ppermute | solution.py:17
  65.5 1.3 copy-start.4
  66.4 28.3 %collective-permute-start.5 = (bf16[4,196,384]{2,0,1:T(4,128)(2,1)}, bf16[4,196,384]{2,0,1:T(4,128)(2,1)S(1)}, u32[]{:S(2)}, u32[]{:S(2)}) collective-permute-start(bf16[4,196,384]{2,0,1:T(4,128)(2,1)} %collective-permute-done.3), channel_id=1, source_target_pairs={{0,14},{2,0},{4,2},{6,4},{8,6},{10,8},{12,10},{14,12},{1,15},{3,1}... | collective-permute-start | bytes 1806344 | tf_op jit(solution)/shard_map/ppermute | solution.py:20
  88.5 13.7 %collective-permute-start.6 = (bf16[4,196,384]{2,0,1:T(4,128)(2,1)S(1)}, bf16[4,196,384]{2,0,1:T(4,128)(2,1)S(1)}, u32[]{:S(2)}, u32[]{:S(2)}) collective-permute-start(bf16[4,196,384]{2,0,1:T(4,128)(2,1)S(1)} %collective-permute-done.4), channel_id=1, source_target_pairs={{0,2},{2,4},{4,6},{6,8},{8,10},{10,12},{12,14},{14,0},{1,3},{3,5},... | collective-permute-start | bytes 1806344 | tf_op jit(solution)/shard_map/ppermute | solution.py:17
  104.8 97.5 %all-gather.5.cloned.1.call-start = ((), (), s32[]{:S(2)}) async-start(), calls=%async_computation.1 | async-start | bytes 5529600 | tf_op jit(solution)/shard_map/all_gather | solution.py:118
  124.3 1.8 copy-start.1
  127.9 8.1 %copy-start.5 = (f32[768]{0:T(1024)S(1)}, f32[768]{0:T(1024)}, u32[]{:S(2)}) copy-start(f32[768]{0:T(1024)} %param.16) | copy-start | bytes 9220
  138.8 3.3 %copy-start.9 = (bf16[768,768]{1,0:T(8,128)(2,1)S(1)}, bf16[768,768]{1,0:T(8,128)(2,1)}, u32[]{:S(2)}) copy-start(bf16[768,768]{1,0:T(8,128)(2,1)} %param.19) | copy-start | bytes 3538948
  145.6 6.5 %copy-start.6 = (f32[768]{0:T(1024)S(1)}, f32[768]{0:T(1024)}, u32[]{:S(2)}) copy-start(f32[768]{0:T(1024)} %param.15) | copy-start | bytes 9220
  152.1 4.3 %copy-start.10 = (bf16[768,768]{1,0:T(8,128)(2,1)S(1)}, bf16[768,768]{1,0:T(8,128)(2,1)}, u32[]{:S(2)}) copy-start(bf16[768,768]{1,0:T(8,128)(2,1)} %param.17) | copy-start | bytes 3538948
  183.9 4.3 %copy-start.13 = (s32[8]{0:T(128)S(1)}, s32[8]{0:T(128)}, u32[]{:S(2)}) copy-start(s32[8]{0:T(128)} %param.27) | copy-start | bytes 100
  183.9 5.6 %copy-start.8 = (f32[1024]{0:T(1024)S(1)}, f32[1024]{0:T(1024)}, u32[]{:S(2)}) copy-start(f32[1024]{0:T(1024)} %param.23) | copy-start | bytes 12292
  183.9 18.4 %copy-start.11 = (bf16[768,768]{1,0:T(8,128)(2,1)S(1)}, bf16[768,768]{1,0:T(8,128)(2,1)}, u32[]{:S(2)}) copy-start(bf16[768,768]{1,0:T(8,128)(2,1)} %param.20) | copy-start | bytes 3538948
  188.1 138.4 %all-reduce.3.cloned.1.call-start = ((), (), s32[]{:S(2)}) async-start(), calls=%async_computation.2 | async-start | bytes 262144
  207.5 11.7 %slice-start = ((s8[4816896]{0:T(1024)(128)(4,1)}), s8[622592]{0:T(1024)(128)(4,1)S(1)}, s32[]{:S(2)}) async-start(s8[4816896]{0:T(1024)(128)(4,1)} %bitcast.58), calls=%async_computation.3 | async-start | bytes 1245184
  212.2 7.0 %slice-start.1 = ((s8[4816896]{0:T(1024)(128)(4,1)}), s8[4194304]{0:T(1024)(128)(4,1)S(1)}, s32[]{:S(2)}) async-start(s8[4816896]{0:T(1024)(128)(4,1)} %bitcast.58), calls=%async_computation.4 | async-start | bytes 8388608
  212.3 7.0 %copy-start.7 = (f32[768]{0:T(1024)S(1)}, f32[768]{0:T(1024)}, u32[]{:S(2)}) copy-start(f32[768]{0:T(1024)} %param.21) | copy-start | bytes 9220
  219.3 5.2 %copy-start.12 = (bf16[4,1024]{1,0:T(4,128)(2,1)S(1)}, bf16[4,1024]{1,0:T(4,128)(2,1)}, u32[]{:S(2)}) copy-start(bf16[4,1024]{1,0:T(4,128)(2,1)} %param.24) | copy-start | bytes 24580
  224.4 11.6 %copy-start.14 = (u32[32]{0:T(128)S(1)}, u32[32]{0:T(128)}, u32[]{:S(2)}) copy-start(u32[32]{0:T(128)} %constant.131) | copy-start | bytes 388
Sparse Core Ops, SparseCore 0:
  105.0 15.7 all-gather.2
  188.3 14.0 all-gather.4
  236.1 90.3 all-reduce.2
